TPU v7x, 128 devices: a whole 4x4x4 slice. The times are simulated.
128 devices in a mesh: energy: 32 (over y, x_hi, z), tile: 4 (over x_lo, core).
Axes of the slice: x: 4 (x_hi: 2, x_lo: 2; x = x_hi * 2 + x_lo), y: 4, z: 4, core: 2. Of those that a mesh axis runs over, the one named last changes fastest.
Arguments:
- gr_electron: bfloat16 [128, 2, 512, 512], P(('energy', 'tile')), may hold values from -0.1875 to 0.1875
- self_lesser: bfloat16 [128, 2, 512, 512], P(('energy', 'tile')), may hold values from -6 to 6
- self_greater: bfloat16 [128, 2, 512, 512], P(('energy', 'tile')), may hold values from -6 to 6
- gr_boson: bfloat16 [128, 2, 512, 512], P(('energy', 'tile')), may hold values from -0.1875 to 0.1875
Outputs:
- lesser_new: bfloat16 [128, 2, 512, 512], P(('energy', 'tile'))
All inputs are finite; a program needn't handle non-finite values.
Results may differ from a plain program's by a relative error of at most 0.025.
Values may be sent and summed in bfloat16 or wider, within the bound.
A program may use at most 64 MiB of HBM per device.

v0:
```python
import functools
import math

import jax
import jax.numpy as jnp
import numpy as np
from jax import lax
from jax.experimental import pallas as pl
from jax.experimental.pallas import tpu as pltpu
from jax.sharding import PartitionSpec as P

MESH = pl.DeviceIdType.MESH
ROWS = 8
LANES = 128
BF16 = jnp.bfloat16
F32 = jnp.float32
PHASES = 4


class Plan:
    def __init__(self, n_energy, n_tile, width):
        self.n_energy, self.n_tile, self.width = n_energy, n_tile, width
        self.devices = n_energy * n_tile
        self.ny = 4 if n_energy % 4 == 0 else 2
        self.nxh = 2 if n_energy // self.ny == 8 else 1
        self.nz = n_energy // (self.ny * self.nxh)
        self.nxl = 2 if n_tile == 4 else 1
        self.nc = n_tile // self.nxl
        self.nx = self.nxh * self.nxl
        self.row_tiles = n_energy
        self.col_tiles = n_tile
        self.half = width // 2
        assert self.half == n_energy * ROWS and width == n_tile * LANES


class Partners:
    def __init__(self, plan):
        self.plan = plan
        e, t = lax.axis_index("energy"), lax.axis_index("tile")
        y = e // (plan.nxh * plan.nz)
        x = (e // plan.nz) % plan.nxh * plan.nxl + t // plan.nc
        self.z, self.c = e % plan.nz, t % plan.nc
        self.sign = 1 - 2 * self.c
        self.y_terms = [(y + plan.ny + self.sign * j) % plan.ny * (plan.nxh * plan.nz) for j in range(plan.ny)]
        xs = [(x + plan.nx + self.sign * j) % plan.nx for j in range(plan.nx)]
        self.xh_terms = [v // plan.nxl * plan.nz for v in xs]
        self.xl_terms = [v % plan.nxl * plan.nc for v in xs]

    def block(self, j, skip, act):
        plan = self.plan
        z = (self.z + plan.nz + self.sign * (j % plan.nz)) % plan.nz
        c = (self.c + j // plan.nz) % plan.nc
        for jx in range(plan.nx):
            for jy in range(plan.ny):
                if skip and jx == 0 and jy == 0:
                    continue
                act(self.y_terms[jy] + self.xh_terms[jx] + z, self.xl_terms[jx] + c)

    def each(self, act):
        self.block(0, True, act)
        if self.plan.nz * self.plan.nc > 1:

            @pl.loop(1, self.plan.nz * self.plan.nc)
            def _(j):
                self.block(j, False, act)


def kernel(
    plan,
    scale,
    gre_hbm,
    sl_hbm,
    sg_hbm,
    grb_hbm,
    fwd_hbm,
    inv_hbm,
    result,
    r_e,
    r_b,
    mid,
    fwd,
    inv,
    pair_out,
    pair_in,
    screen_out,
    screen_in,
    polar_out,
    polar_in,
    self_out,
    self_in,
    wide,
    back_wide,
    spec_l,
    left_sum,
    in_sem,
    send_sem,
    recv_sem,
):
    width, half, dev = plan.width, plan.half, plan.devices
    me_e, me_t = lax.axis_index("energy"), lax.axis_index("tile")
    me = me_e * plan.n_tile + me_t
    partners = Partners(plan)
    scope = jax.named_scope

    def load(src, dst, k):
        copy = pltpu.make_async_copy(src, dst, in_sem.at[k])
        copy.start()
        return copy

    lo, hi = pl.ds(0, width), pl.ds(width, width)

    def load_matrix(src, dst, k):
        return [
            load(src.at[0, 0], dst.at[lo, lo], k),
            load(src.at[0, 1], dst.at[lo, hi], k + 1),
            load(src.at[0, 0], dst.at[hi, hi], k + 2),
        ]

    loads_r = load_matrix(gre_hbm, r_e, 0)
    loads_l = load_matrix(sl_hbm, mid.at[0], 3)
    loads_g = load_matrix(sg_hbm, mid.at[1], 6)
    loads_t = [load(fwd_hbm, fwd, 9), load(inv_hbm, inv, 10)]
    loads_b = load_matrix(grb_hbm, r_b, 11)

    barrier = pltpu.get_barrier_semaphore()

    with scope("signal"):
        partners.each(lambda e, t: pl.semaphore_signal(barrier, inc=1, device_id=(e, t), device_id_type=MESH))

    def negate(ref):
        ref[width:, :width] = -ref[:width, width:]

    def right_product(left, outer):
        return lax.dot_general(left, outer[...], (((1,), (1,)), ((), ())), preferred_element_type=F32)

    def rows_of(h):
        return pl.ds(h * half, half)

    def sandwich_half(outer, middle, h):
        left = jnp.dot(outer[rows_of(h), :], middle[...], preferred_element_type=F32).astype(BF16)
        return right_product(left, outer)

    def left_part(outer, middle, rows, h):
        cols = (rows_of(h), pl.ds(width + h * half, half))
        return sum(jnp.dot(outer[rows, k], middle[k, :], preferred_element_type=F32) for k in cols)

    def to_blocks(right, blocks, row0):
        for ct in range(plan.col_tiles):
            pieces = [
                right[:, part * width + ct * LANES : part * width + (ct + 1) * LANES].reshape(
                    plan.row_tiles, ROWS, LANES
                )
                for part in range(2)
            ]
            blocks[:, ct, row0 : row0 + 2 * ROWS, :] = jnp.concatenate(pieces, axis=1).astype(BF16)

    def send(source, own, landing, slot):
        with scope("send"):
            partners.each(
                lambda e, t: pltpu.make_async_remote_copy(
                    src_ref=source(e, t),
                    dst_ref=landing.at[me],
                    send_sem=send_sem.at[slot],
                    recv_sem=recv_sem.at[slot],
                    device_id=(e, t),
                    device_id_type=MESH,
                ).start()
            )
        landing[me] = own

    def send_blocks(blocks, landing, slot):
        send(lambda e, t: blocks.at[e, t], blocks[me_e, me_t], landing, slot)

    def send_energies(blocks, landing, slot):
        send(lambda e, t: blocks.at[e * plan.n_tile + t], blocks[me], landing, slot)

    def wait_for(landing, sem, slot):
        view = landing.at[pl.ds(0, dev - 1)]
        pltpu.make_async_copy(view, view, sem.at[slot]).wait()

    step = 8

    def widen(landing, rows):
        @pl.loop(0, dev // step)
        def _(i):
            block = landing[pl.ds(i * step, step)].astype(F32)
            start = pl.multiple_of(i * step * rows, 8)
            wide[pl.ds(start, step * rows), :] = block.reshape(step * rows, LANES)

    group = 4
    length = 2 * dev

    def spectrum(g, first, rows):
        x = jnp.concatenate(
            [
                jnp.concatenate(
                    [
                        wide[pl.ds(first + part * ROWS + g * group + i, dev, stride=rows), :].astype(BF16)
                        for part in range(2)
                    ],
                    axis=0,
                )
                for i in range(group)
            ],
            axis=1,
        )
        return jnp.dot(fwd[...], x, preferred_element_type=F32)

    def back(g, p_re, p_im):
        p = jnp.concatenate([p_re.astype(BF16), p_im.astype(BF16)], axis=0)
        field = jnp.dot(inv[...], p, preferred_element_type=F32) * scale
        for i in range(group):
            for part in range(2):
                back_wide[pl.ds(part * ROWS + g * group + i, dev, stride=2 * ROWS), :] = field[
                    part * dev : (part + 1) * dev, i * LANES : (i + 1) * LANES
                ]

    def narrow(blocks):
        @pl.loop(0, dev // step)
        def _(i):
            start = pl.multiple_of(i * step * 2 * ROWS, 8)
            block = back_wide[pl.ds(start, step * 2 * ROWS), :].astype(BF16)
            blocks[pl.ds(i * step, step)] = block.reshape(step, 2 * ROWS, LANES)

    def lanes_of(h, g):
        start = (h * ROWS + g * group) * LANES
        return slice(start, start + group * LANES)

    def polar_half(h):
        widen(pair_in.at[h], 4 * ROWS)
        for g in range(ROWS // group):
            spec = spectrum(g, 0, 4 * ROWS)
            spec_l[:, lanes_of(h, g)] = spec
            l_re, l_im = spec[:length], spec[length:]
            spec = spectrum(g, 2 * ROWS, 4 * ROWS)
            g_re, g_im = spec[:length], spec[length:]
            back(g, l_re * g_re + l_im * g_im, l_im * g_re - l_re * g_im)
        narrow(polar_out.at[h])

    def self_half(h):
        widen(screen_in.at[h], 2 * ROWS)
        for g in range(ROWS // group):
            spec = spectrum(g, 0, 2 * ROWS)
            s_re, s_im = spec[:length], spec[length:]
            l_re, l_im = spec_l[:length, lanes_of(h, g)], spec_l[length:, lanes_of(h, g)]
            back(g, l_re * s_re - l_im * s_im, l_re * s_im + l_im * s_re)
        narrow(self_out.at[h])

    def assemble(landing, dst, h):
        rows, rows_low = rows_of(h), pl.ds(width + h * half, half)
        for ct in range(plan.col_tiles):
            tiles = jnp.concatenate(
                [landing[pl.ds(rt * plan.n_tile + ct, 1)] for rt in range(plan.row_tiles)], axis=0
            ).astype(F32)
            real = tiles[:, :ROWS, :].reshape(half, LANES).astype(BF16)
            imag = tiles[:, ROWS:, :].reshape(half, LANES).astype(BF16)
            cols, cols_im = slice(ct * LANES, (ct + 1) * LANES), slice(width + ct * LANES, width + (ct + 1) * LANES)
            dst[rows, cols] = real
            dst[rows_low, cols_im] = real
            dst[rows, cols_im] = imag
            dst[rows_low, cols] = -imag

    with scope("load"):
        for copy in loads_r + loads_l + loads_g:
            copy.wait()
        negate(r_e)
        negate(mid.at[0])
        negate(mid.at[1])
    for h in range(2):
        with scope("pair"):
            to_blocks(sandwich_half(r_e, mid.at[0], h), pair_out.at[h], 0)
            to_blocks(sandwich_half(r_e, mid.at[1], h), pair_out.at[h], 2 * ROWS)
        if h == 0:
            with scope("meet"):
                pl.semaphore_wait(barrier, dev - 1)
        send_blocks(pair_out.at[h], pair_in.at[h], h)
    with scope("load2"):
        for copy in loads_t + loads_b:
            copy.wait()
        negate(r_b)

    for h in range(2):
        with scope("wait_pair"):
            wait_for(pair_in.at[h], recv_sem, h)
        with scope("polar"):
            polar_half(h)
        send_energies(polar_out.at[h], polar_in.at[h], 2 + h)

    with scope("wait_polar"):
        wait_for(polar_in.at[0], recv_sem, 2)
    with scope("left_polar"):
        assemble(polar_in.at[0], mid.at[2], 0)
        left_sum[...] = left_part(r_b, mid.at[2], pl.ds(0, width), 0)
    with scope("wait_polar"):
        wait_for(polar_in.at[1], recv_sem, 3)
    with scope("left_polar"):
        assemble(polar_in.at[1], mid.at[2], 1)
    for h in range(2):
        with scope("screened"):
            left = (left_sum[rows_of(h), :] + left_part(r_b, mid.at[2], rows_of(h), 1)).astype(BF16)
            to_blocks(right_product(left, r_b), screen_out.at[h], 0)
        send_blocks(screen_out.at[h], screen_in.at[h], 4 + h)

    for h in range(2):
        with scope("wait_screened"):
            wait_for(screen_in.at[h], recv_sem, 4 + h)
        with scope("self_energy"):
            self_half(h)
        send_energies(self_out.at[h], self_in.at[h], 6 + h)

    with scope("wait_self"):
        wait_for(self_in.at[0], recv_sem, 6)
    with scope("left_self"):
        assemble(self_in.at[0], mid.at[3], 0)
        left_sum[...] = left_part(r_e, mid.at[3], pl.ds(0, width), 0)
    with scope("wait_self"):
        wait_for(self_in.at[1], recv_sem, 7)
    with scope("lesser_new"):
        assemble(self_in.at[1], mid.at[3], 1)
        for h in range(2):
            left = (left_sum[rows_of(h), :] + left_part(r_e, mid.at[3], rows_of(h), 1)).astype(BF16)
            right = right_product(left, r_e).astype(BF16)
            for part in range(2):
                result[0, part, h * half : (h + 1) * half, :] = right[:, part * width : (part + 1) * width]
    with scope("finish"):
        for slot in range(2 * PHASES):
            landing = (pair_in, polar_in, screen_in, self_in)[slot // 2]
            wait_for(landing.at[slot % 2], send_sem, slot)


def tables(n):
    length = 2 * n
    phase = np.arange(length)[:, None] * np.arange(n)[None, :] % length
    angle = phase * (2.0 * math.pi / length)
    cosine, sine = np.cos(angle), np.sin(angle)
    forward = np.block([[cosine, sine], [-sine, cosine]])
    return forward.astype(np.float32), forward.T.astype(np.float32)


def shards(plan, gr_electron, self_lesser, self_greater, gr_boson):
    width, dev = plan.width, plan.devices
    forward, inverse = tables(dev)
    scale = 1.0 / (2 * dev * math.sqrt(dev))
    any_spec = pl.BlockSpec(memory_space=pl.ANY)

    def by_owner(rows):
        return pltpu.VMEM((2, plan.row_tiles, plan.col_tiles, rows, LANES), BF16)

    def by_energy(rows):
        return pltpu.VMEM((2, dev, rows, LANES), BF16)

    return pl.pallas_call(
        functools.partial(kernel, plan, scale),
        out_shape=pltpu.VMEM((1, 2, width, width), BF16),
        in_specs=[any_spec] * 6,
        out_specs=pl.BlockSpec(memory_space=pltpu.VMEM),
        scratch_shapes=[
            pltpu.VMEM((2 * width, 2 * width), BF16),
            pltpu.VMEM((2 * width, 2 * width), BF16),
            pltpu.VMEM((4, 2 * width, 2 * width), BF16),
            pltpu.VMEM((4 * dev, 2 * dev), BF16),
            pltpu.VMEM((2 * dev, 4 * dev), BF16),
            by_owner(4 * ROWS),
            by_energy(4 * ROWS),
            by_owner(2 * ROWS),
            by_energy(2 * ROWS),
            by_energy(2 * ROWS),
            by_energy(2 * ROWS),
            by_energy(2 * ROWS),
            by_energy(2 * ROWS),
            pltpu.VMEM((dev * 4 * ROWS, LANES), F32),
            pltpu.VMEM((dev * 2 * ROWS, LANES), F32),
            pltpu.VMEM((4 * dev, 2 * ROWS * LANES), F32),
            pltpu.VMEM((width, 2 * width), F32),
            pltpu.SemaphoreType.DMA((14,)),
            pltpu.SemaphoreType.DMA((2 * PHASES,)),
            pltpu.SemaphoreType.DMA((2 * PHASES,)),
        ],
        compiler_params=pltpu.CompilerParams(
            collective_id=0, has_side_effects=True, vmem_limit_bytes=56 * 1024 * 1024
        ),
        name="gw_step",
    )(
        gr_electron,
        self_lesser,
        self_greater,
        gr_boson,
        jnp.asarray(forward).astype(BF16),
        jnp.asarray(inverse).astype(BF16),
    )


def solution(mesh):
    def step(gr_electron, self_lesser, self_greater, gr_boson):
        plan = Plan(mesh.shape["energy"], mesh.shape["tile"], gr_electron.shape[3])
        return shards(plan, gr_electron, self_lesser, self_greater, gr_boson)

    spec = P(("energy", "tile"), None, None, None)
    return jax.shard_map(step, mesh=mesh, in_specs=(spec,) * 4, out_specs=spec, check_vma=False)
```

profile of v0, /device:TPU:1, one launch (start us, length us, event | category | flops | bytes accessed | tf_op | source)
XLA Modules:
  0.0 86.1 jit_solution(12629087219214789697)
XLA Ops:
  0.0 85.1 %gw_step.1 = bf16[1,2,512,512]{3,2,1,0:T(8,128)(2,1)S(1)} custom-call(bf16[1,2,512,512]{3,2,1,0:T(8,128)(2,1)} %gre_hbm.1, bf16[1,2,512,512]{3,2,1,0:T(8,128)(2,1)} %sl_hbm.1, bf16[1,2,512,512]{3,2,1,0:T(8,128)(2,1)} %sg_hbm.1, bf16[1,2,512,512]{3,2,1,0:T(8,128)(2,1)} %grb_hbm.1, bf16[512,256]{1,0:T(8,128)(2,1)} %constant.10.fwd_hbm, ...), custom_call_target="tpu_custom_call" | custom-call | tf_op jit(solution)/shard_map/gw_step/pallas_call | solution.py:352
  85.1 1.0 %copy.8 = bf16[1,2,512,512]{3,2,1,0:T(8,128)(2,1)} copy(bf16[1,2,512,512]{3,2,1,0:T(8,128)(2,1)S(1)} %gw_step.1) | data formatting | bytes 2097152
where the time goes:
time: 86.2 us; the launch traced here: 86.1 us
  Pallas kernels  85.1 us (99%)
  local copies, waits for them, and re-layouts  0.97 us (1%)
    pallas_call x1, Pallas kernels, shards(): pl.pallas_call(functools.partial(kernel, plan, scale), out_shape=pltpu.VM...  85.1 us

commit v1 on v0

--- a/solution.py
+++ b/solution.py
@@ -1,4 +1,5 @@
 import functools
+import itertools
 import math
 
 import jax
@@ -39,30 +40,25 @@
         e, t = lax.axis_index("energy"), lax.axis_index("tile")
         y = e // (plan.nxh * plan.nz)
         x = (e // plan.nz) % plan.nxh * plan.nxl + t // plan.nc
-        self.z, self.c = e % plan.nz, t % plan.nc
-        self.sign = 1 - 2 * self.c
-        self.y_terms = [(y + plan.ny + self.sign * j) % plan.ny * (plan.nxh * plan.nz) for j in range(plan.ny)]
-        xs = [(x + plan.nx + self.sign * j) % plan.nx for j in range(plan.nx)]
+        z, c = e % plan.nz, t % plan.nc
+        sign = 1 - 2 * c
+        self.y_terms = [(y + plan.ny + sign * j) % plan.ny * (plan.nxh * plan.nz) for j in range(plan.ny)]
+        xs = [(x + plan.nx + sign * j) % plan.nx for j in range(plan.nx)]
         self.xh_terms = [v // plan.nxl * plan.nz for v in xs]
         self.xl_terms = [v % plan.nxl * plan.nc for v in xs]
-
-    def block(self, j, skip, act):
-        plan = self.plan
-        z = (self.z + plan.nz + self.sign * (j % plan.nz)) % plan.nz
-        c = (self.c + j // plan.nz) % plan.nc
-        for jx in range(plan.nx):
-            for jy in range(plan.ny):
-                if skip and jx == 0 and jy == 0:
-                    continue
-                act(self.y_terms[jy] + self.xh_terms[jx] + z, self.xl_terms[jx] + c)
+        self.c_terms = [(c + j) % plan.nc for j in range(plan.nc)]
+        self.z_terms = [(z + plan.nz + sign * j) % plan.nz for j in range(plan.nz)]
+
+        def hops(j, n):
+            return min(j, n - j)
+
+        sizes = (plan.nc, plan.nz, plan.nx, plan.ny)
+        others = list(itertools.product(*map(range, sizes)))[1:]
+        self.order = sorted(others, key=lambda p: (-sum(map(hops, p[1:], sizes[1:])), -p[0]))
 
     def each(self, act):
-        self.block(0, True, act)
-        if self.plan.nz * self.plan.nc > 1:
-
-            @pl.loop(1, self.plan.nz * self.plan.nc)
-            def _(j):
-                self.block(j, False, act)
+        for jc, jz, jx, jy in self.order:
+            act(self.y_terms[jy] + self.xh_terms[jx] + self.z_terms[jz], self.xl_terms[jx] + self.c_terms[jc])
 
 
 def kernel(
@@ -110,25 +106,20 @@
     lo, hi = pl.ds(0, width), pl.ds(width, width)
 
     def load_matrix(src, dst, k):
-        return [
-            load(src.at[0, 0], dst.at[lo, lo], k),
-            load(src.at[0, 1], dst.at[lo, hi], k + 1),
-            load(src.at[0, 0], dst.at[hi, hi], k + 2),
-        ]
+        return [load(src.at[0, 0], dst.at[lo, lo], k), load(src.at[0, 1], dst.at[lo, hi], k + 1)]
 
     loads_r = load_matrix(gre_hbm, r_e, 0)
-    loads_l = load_matrix(sl_hbm, mid.at[0], 3)
-    loads_g = load_matrix(sg_hbm, mid.at[1], 6)
-    loads_t = [load(fwd_hbm, fwd, 9), load(inv_hbm, inv, 10)]
-    loads_b = load_matrix(grb_hbm, r_b, 11)
+    loads_l = load_matrix(sl_hbm, mid.at[0], 2)
+    loads_g = load_matrix(sg_hbm, mid.at[1], 4)
 
     barrier = pltpu.get_barrier_semaphore()
 
     with scope("signal"):
         partners.each(lambda e, t: pl.semaphore_signal(barrier, inc=1, device_id=(e, t), device_id_type=MESH))
 
-    def negate(ref):
+    def complete(ref):
         ref[width:, :width] = -ref[:width, width:]
+        ref[width:, width:] = ref[:width, :width]
 
     def right_product(left, outer):
         return lax.dot_general(left, outer[...], (((1,), (1,)), ((), ())), preferred_element_type=F32)
@@ -154,7 +145,13 @@
             ]
             blocks[:, ct, row0 : row0 + 2 * ROWS, :] = jnp.concatenate(pieces, axis=1).astype(BF16)
 
+    def landings(slot):
+        return (pair_in, polar_in, screen_in, self_in)[slot // 2].at[slot % 2]
+
     def send(source, own, landing, slot):
+        if slot > 0:
+            with scope("gate"):
+                wait_for(landings(slot - 1), send_sem, slot - 1)
         with scope("send"):
             partners.each(
                 lambda e, t: pltpu.make_async_remote_copy(
@@ -178,75 +175,67 @@
         view = landing.at[pl.ds(0, dev - 1)]
         pltpu.make_async_copy(view, view, sem.at[slot]).wait()
 
-    step = 8
-
-    def widen(landing, rows):
+    step = min(16, dev)
+    length = 2 * dev
+    pair_pitch, field_pitch = 4 * ROWS + 8, 2 * ROWS + 8
+
+    def widen(landing, rows, pitch):
         @pl.loop(0, dev // step)
         def _(i):
-            block = landing[pl.ds(i * step, step)].astype(F32)
-            start = pl.multiple_of(i * step * rows, 8)
-            wide[pl.ds(start, step * rows), :] = block.reshape(step * rows, LANES)
-
-    group = 4
-    length = 2 * dev
-
-    def spectrum(g, first, rows):
+            for k in range(step):
+                start = pl.multiple_of((i * step + k) * pitch, 8)
+                wide[pl.ds(start, rows), :] = landing[i * step + k].astype(F32)
+
+    def spectrum(first, pitch):
         x = jnp.concatenate(
             [
                 jnp.concatenate(
                     [
-                        wide[pl.ds(first + part * ROWS + g * group + i, dev, stride=rows), :].astype(BF16)
+                        wide[pl.ds(first + part * ROWS + i, dev, stride=pitch), :].astype(BF16)
                         for part in range(2)
                     ],
                     axis=0,
                 )
-                for i in range(group)
+                for i in range(ROWS)
             ],
             axis=1,
         )
-        return jnp.dot(fwd[...], x, preferred_element_type=F32)
-
-    def back(g, p_re, p_im):
+        spec = jnp.dot(fwd[...], x, preferred_element_type=F32)
+        return spec[:length], spec[length:]
+
+    def back(p_re, p_im, blocks):
         p = jnp.concatenate([p_re.astype(BF16), p_im.astype(BF16)], axis=0)
         field = jnp.dot(inv[...], p, preferred_element_type=F32) * scale
-        for i in range(group):
+        for i in range(ROWS):
             for part in range(2):
-                back_wide[pl.ds(part * ROWS + g * group + i, dev, stride=2 * ROWS), :] = field[
+                back_wide[pl.ds(part * ROWS + i, dev, stride=field_pitch), :] = field[
                     part * dev : (part + 1) * dev, i * LANES : (i + 1) * LANES
                 ]
 
-    def narrow(blocks):
         @pl.loop(0, dev // step)
         def _(i):
-            start = pl.multiple_of(i * step * 2 * ROWS, 8)
-            block = back_wide[pl.ds(start, step * 2 * ROWS), :].astype(BF16)
-            blocks[pl.ds(i * step, step)] = block.reshape(step, 2 * ROWS, LANES)
-
-    def lanes_of(h, g):
-        start = (h * ROWS + g * group) * LANES
-        return slice(start, start + group * LANES)
+            for k in range(step):
+                start = pl.multiple_of((i * step + k) * field_pitch, 8)
+                blocks[i * step + k] = back_wide[pl.ds(start, 2 * ROWS), :].astype(BF16)
+
+    def lanes_of(h):
+        return slice(h * ROWS * LANES, (h + 1) * ROWS * LANES)
 
     def polar_half(h):
-        widen(pair_in.at[h], 4 * ROWS)
-        for g in range(ROWS // group):
-            spec = spectrum(g, 0, 4 * ROWS)
-            spec_l[:, lanes_of(h, g)] = spec
-            l_re, l_im = spec[:length], spec[length:]
-            spec = spectrum(g, 2 * ROWS, 4 * ROWS)
-            g_re, g_im = spec[:length], spec[length:]
-            back(g, l_re * g_re + l_im * g_im, l_im * g_re - l_re * g_im)
-        narrow(polar_out.at[h])
+        widen(pair_in.at[h], 4 * ROWS, pair_pitch)
+        l_re, l_im = spectrum(0, pair_pitch)
+        spec_l[:length, lanes_of(h)] = l_re
+        spec_l[length:, lanes_of(h)] = l_im
+        g_re, g_im = spectrum(2 * ROWS, pair_pitch)
+        back(l_re * g_re + l_im * g_im, l_im * g_re - l_re * g_im, polar_out.at[h])
 
     def self_half(h):
-        widen(screen_in.at[h], 2 * ROWS)
-        for g in range(ROWS // group):
-            spec = spectrum(g, 0, 2 * ROWS)
-            s_re, s_im = spec[:length], spec[length:]
-            l_re, l_im = spec_l[:length, lanes_of(h, g)], spec_l[length:, lanes_of(h, g)]
-            back(g, l_re * s_re - l_im * s_im, l_re * s_im + l_im * s_re)
-        narrow(self_out.at[h])
-
-    def assemble(landing, dst, h):
+        widen(screen_in.at[h], 2 * ROWS, field_pitch)
+        s_re, s_im = spectrum(0, field_pitch)
+        l_re, l_im = spec_l[:length, lanes_of(h)], spec_l[length:, lanes_of(h)]
+        back(l_re * s_re - l_im * s_im, l_re * s_im + l_im * s_re, self_out.at[h])
+
+    def assemble(landing, dst, h, lower):
         rows, rows_low = rows_of(h), pl.ds(width + h * half, half)
         for ct in range(plan.col_tiles):
             tiles = jnp.concatenate(
@@ -256,28 +245,35 @@
             imag = tiles[:, ROWS:, :].reshape(half, LANES).astype(BF16)
             cols, cols_im = slice(ct * LANES, (ct + 1) * LANES), slice(width + ct * LANES, width + (ct + 1) * LANES)
             dst[rows, cols] = real
-            dst[rows_low, cols_im] = real
             dst[rows, cols_im] = imag
-            dst[rows_low, cols] = -imag
+            if lower:
+                dst[rows_low, cols_im] = real
+                dst[rows_low, cols] = -imag
 
     with scope("load"):
-        for copy in loads_r + loads_l + loads_g:
+        for copy in loads_r + loads_l:
             copy.wait()
-        negate(r_e)
-        negate(mid.at[0])
-        negate(mid.at[1])
+        complete(r_e)
+        complete(mid.at[0])
+    later = []
     for h in range(2):
         with scope("pair"):
             to_blocks(sandwich_half(r_e, mid.at[0], h), pair_out.at[h], 0)
+            if h == 0:
+                for copy in loads_g:
+                    copy.wait()
+                complete(mid.at[1])
             to_blocks(sandwich_half(r_e, mid.at[1], h), pair_out.at[h], 2 * ROWS)
         if h == 0:
             with scope("meet"):
                 pl.semaphore_wait(barrier, dev - 1)
         send_blocks(pair_out.at[h], pair_in.at[h], h)
+        if h == 0:
+            later = [load(fwd_hbm, fwd, 6), load(inv_hbm, inv, 7)] + load_matrix(grb_hbm, r_b, 8)
     with scope("load2"):
-        for copy in loads_t + loads_b:
+        for copy in later:
             copy.wait()
-        negate(r_b)
+        complete(r_b)
 
     for h in range(2):
         with scope("wait_pair"):
@@ -289,12 +285,12 @@
     with scope("wait_polar"):
         wait_for(polar_in.at[0], recv_sem, 2)
     with scope("left_polar"):
-        assemble(polar_in.at[0], mid.at[2], 0)
+        assemble(polar_in.at[0], mid.at[2], 0, True)
         left_sum[...] = left_part(r_b, mid.at[2], pl.ds(0, width), 0)
     with scope("wait_polar"):
         wait_for(polar_in.at[1], recv_sem, 3)
     with scope("left_polar"):
-        assemble(polar_in.at[1], mid.at[2], 1)
+        assemble(polar_in.at[1], mid.at[2], 1, True)
     for h in range(2):
         with scope("screened"):
             left = (left_sum[rows_of(h), :] + left_part(r_b, mid.at[2], rows_of(h), 1)).astype(BF16)
@@ -308,24 +304,27 @@
             self_half(h)
         send_energies(self_out.at[h], self_in.at[h], 6 + h)
 
+    def right_first(h):
+        assemble(self_in.at[h], mid.at[0], h, False)
+        right = right_product(mid[0, rows_of(h), :], r_e).astype(BF16)
+        mid[1, rows_of(h), :] = right
+        low = pl.ds(width + h * half, half)
+        mid[1, low, :width] = -right[:, width:]
+        mid[1, low, width:] = right[:, :width]
+        return left_part(r_e, mid.at[1], pl.ds(0, width), h)
+
     with scope("wait_self"):
         wait_for(self_in.at[0], recv_sem, 6)
-    with scope("left_self"):
-        assemble(self_in.at[0], mid.at[3], 0)
-        left_sum[...] = left_part(r_e, mid.at[3], pl.ds(0, width), 0)
+    with scope("right_self"):
+        left_sum[...] = right_first(0)
     with scope("wait_self"):
         wait_for(self_in.at[1], recv_sem, 7)
     with scope("lesser_new"):
-        assemble(self_in.at[1], mid.at[3], 1)
-        for h in range(2):
-            left = (left_sum[rows_of(h), :] + left_part(r_e, mid.at[3], rows_of(h), 1)).astype(BF16)
-            right = right_product(left, r_e).astype(BF16)
-            for part in range(2):
-                result[0, part, h * half : (h + 1) * half, :] = right[:, part * width : (part + 1) * width]
+        total = (left_sum[...] + right_first(1)).astype(BF16)
+        for part in range(2):
+            result[0, part] = total[:, part * width : (part + 1) * width]
     with scope("finish"):
-        for slot in range(2 * PHASES):
-            landing = (pair_in, polar_in, screen_in, self_in)[slot // 2]
-            wait_for(landing.at[slot % 2], send_sem, slot)
+        wait_for(landings(2 * PHASES - 1), send_sem, 2 * PHASES - 1)
 
 
 def tables(n):
@@ -357,7 +356,7 @@
         scratch_shapes=[
             pltpu.VMEM((2 * width, 2 * width), BF16),
             pltpu.VMEM((2 * width, 2 * width), BF16),
-            pltpu.VMEM((4, 2 * width, 2 * width), BF16),
+            pltpu.VMEM((3, 2 * width, 2 * width), BF16),
             pltpu.VMEM((4 * dev, 2 * dev), BF16),
             pltpu.VMEM((2 * dev, 4 * dev), BF16),
             by_owner(4 * ROWS),
@@ -368,11 +367,11 @@
             by_energy(2 * ROWS),
             by_energy(2 * ROWS),
             by_energy(2 * ROWS),
-            pltpu.VMEM((dev * 4 * ROWS, LANES), F32),
-            pltpu.VMEM((dev * 2 * ROWS, LANES), F32),
+            pltpu.VMEM((dev * (4 * ROWS + 8), LANES), F32),
+            pltpu.VMEM((dev * (2 * ROWS + 8), LANES), F32),
             pltpu.VMEM((4 * dev, 2 * ROWS * LANES), F32),
             pltpu.VMEM((width, 2 * width), F32),
-            pltpu.SemaphoreType.DMA((14,)),
+            pltpu.SemaphoreType.DMA((10,)),
             pltpu.SemaphoreType.DMA((2 * PHASES,)),
             pltpu.SemaphoreType.DMA((2 * PHASES,)),
         ],

time: 86.2 us -> 86.2 us (level)
  no operation moved by 1% of the time
where the time goes in v1:
time: 86.2 us; the launch traced here: 86.1 us
  Pallas kernels  85.1 us (99%)
  local copies, waits for them, and re-layouts  0.97 us (1%)
    pallas_call x1, Pallas kernels, shards(): pl.pallas_call(functools.partial(kernel, plan, scale), out_shape=pltpu.VM...  85.1 us

profile of v1, /device:TPU:1, one launch (start us, length us, event | category | flops | bytes accessed | tf_op | source)
XLA Modules:
  0.0 86.1 jit_solution(10892901304031097008)
XLA Ops:
  0.0 85.1 %gw_step.1 = bf16[1,2,512,512]{3,2,1,0:T(8,128)(2,1)S(1)} custom-call(bf16[1,2,512,512]{3,2,1,0:T(8,128)(2,1)} %gre_hbm.1, bf16[1,2,512,512]{3,2,1,0:T(8,128)(2,1)} %sl_hbm.1, bf16[1,2,512,512]{3,2,1,0:T(8,128)(2,1)} %sg_hbm.1, bf16[1,2,512,512]{3,2,1,0:T(8,128)(2,1)} %grb_hbm.1, bf16[512,256]{1,0:T(8,128)(2,1)} %constant.10.fwd_hbm, ...), custom_call_target="tpu_custom_call" | custom-call | tf_op jit(solution)/shard_map/gw_step/pallas_call | solution.py:351
  85.1 1.0 %copy.8 = bf16[1,2,512,512]{3,2,1,0:T(8,128)(2,1)} copy(bf16[1,2,512,512]{3,2,1,0:T(8,128)(2,1)S(1)} %gw_step.1) | data formatting | bytes 2097152

commit v2 on v1

--- a/solution.py
+++ b/solution.py
@@ -55,6 +55,15 @@
         sizes = (plan.nc, plan.nz, plan.nx, plan.ny)
         others = list(itertools.product(*map(range, sizes)))[1:]
         self.order = sorted(others, key=lambda p: (-sum(map(hops, p[1:], sizes[1:])), -p[0]))
+
+    def each_by_core(self, act):
+        plan = self.plan
+        chips = [p[1:] for p in self.order if p[0] == 0]
+        for core in range(plan.nc):
+            for jz, jx, jy in chips:
+                act(self.y_terms[jy] + self.xh_terms[jx] + self.z_terms[jz], self.xl_terms[jx] + core)
+            if core == 0 and plan.nc > 1:
+                act(self.y_terms[0] + self.xh_terms[0] + self.z_terms[0], self.xl_terms[0] + self.c_terms[1])
 
     def each(self, act):
         for jc, jz, jx, jy in self.order:
@@ -148,28 +157,31 @@
     def landings(slot):
         return (pair_in, polar_in, screen_in, self_in)[slot // 2].at[slot % 2]
 
-    def send(source, own, landing, slot):
-        if slot > 0:
-            with scope("gate"):
-                wait_for(landings(slot - 1), send_sem, slot - 1)
-        with scope("send"):
-            partners.each(
-                lambda e, t: pltpu.make_async_remote_copy(
-                    src_ref=source(e, t),
-                    dst_ref=landing.at[me],
-                    send_sem=send_sem.at[slot],
-                    recv_sem=recv_sem.at[slot],
-                    device_id=(e, t),
-                    device_id_type=MESH,
-                ).start()
-            )
+    def send(source, own, landing, slot, walk=None):
+        @pl.when(me >= 0)
+        def _():
+            if slot > 0:
+                with scope("gate"):
+                    wait_for(landings(slot - 1), send_sem, slot - 1)
+            with scope("send"):
+                (walk or partners.each)(
+                    lambda e, t: pltpu.make_async_remote_copy(
+                        src_ref=source(e, t),
+                        dst_ref=landing.at[me],
+                        send_sem=send_sem.at[slot],
+                        recv_sem=recv_sem.at[slot],
+                        device_id=(e, t),
+                        device_id_type=MESH,
+                    ).start()
+                )
+
         landing[me] = own
 
     def send_blocks(blocks, landing, slot):
         send(lambda e, t: blocks.at[e, t], blocks[me_e, me_t], landing, slot)
 
-    def send_energies(blocks, landing, slot):
-        send(lambda e, t: blocks.at[e * plan.n_tile + t], blocks[me], landing, slot)
+    def send_energies(blocks, landing, slot, walk=None):
+        send(lambda e, t: blocks.at[e * plan.n_tile + t], blocks[me], landing, slot, walk)
 
     def wait_for(landing, sem, slot):
         view = landing.at[pl.ds(0, dev - 1)]
@@ -280,7 +292,7 @@
             wait_for(pair_in.at[h], recv_sem, h)
         with scope("polar"):
             polar_half(h)
-        send_energies(polar_out.at[h], polar_in.at[h], 2 + h)
+        send_energies(polar_out.at[h], polar_in.at[h], 2 + h, partners.each_by_core)
 
     with scope("wait_polar"):
         wait_for(polar_in.at[0], recv_sem, 2)

time: 86.2 us -> 80.9 us (0.939)
  Pallas kernels: 85.1 us -> 79.8 us
    pallas_call x1, Pallas kernels: 85.1 us -> 79.8 us  [shards(): pl.pallas_call(functools.partial(kernel, plan, scale), out_shape=pltpu.VM...]
where the time goes in v2:
time: 80.9 us; the launch traced here: 80.8 us
  Pallas kernels  79.8 us (99%)
  local copies, waits for them, and re-layouts  0.97 us (1%)
    pallas_call x1, Pallas kernels, shards(): pl.pallas_call(functools.partial(kernel, plan, scale), out_shape=pltpu.VM...  79.8 us

profile of v2, /device:TPU:1, one launch (start us, length us, event | category | flops | bytes accessed | tf_op | source)
XLA Modules:
  0.0 80.8 jit_solution(11530351135129960633)
XLA Ops:
  0.0 79.8 %gw_step.1 = bf16[1,2,512,512]{3,2,1,0:T(8,128)(2,1)S(1)} custom-call(bf16[1,2,512,512]{3,2,1,0:T(8,128)(2,1)} %gre_hbm.1, bf16[1,2,512,512]{3,2,1,0:T(8,128)(2,1)} %sl_hbm.1, bf16[1,2,512,512]{3,2,1,0:T(8,128)(2,1)} %sg_hbm.1, bf16[1,2,512,512]{3,2,1,0:T(8,128)(2,1)} %grb_hbm.1, bf16[512,256]{1,0:T(8,128)(2,1)} %constant.10.fwd_hbm, ...), custom_call_target="tpu_custom_call" | custom-call | tf_op jit(solution)/shard_map/gw_step/pallas_call | solution.py:363
  79.9 1.0 %copy.8 = bf16[1,2,512,512]{3,2,1,0:T(8,128)(2,1)} copy(bf16[1,2,512,512]{3,2,1,0:T(8,128)(2,1)S(1)} %gw_step.1) | data formatting | bytes 2097152
